TPU v7x, 512 devices: a whole 4x8x8 slice. The times are simulated.
512 devices in a mesh: ctx: 64 (over z_lo, y, core), tp: 8 (over x, z_hi).
Axes of the slice: x: 4, y: 8, z: 8 (z_hi: 2, z_lo: 4; z = z_hi * 4 + z_lo), core: 2. Of those that a mesh axis runs over, the one named last changes fastest.
Arguments:
- inputs: float32 [16384, 5120], P('ctx', 'tp'), may hold values from -6 to 6
- state_input: float32 [16384, 128], P('ctx'), may hold values from -0.125 to 0.125
- state_output: float32 [16384, 128], P('ctx'), may hold values from -0.125 to 0.125
- decay_codes: int32 [80, 16384], P('tp', 'ctx'), may hold values from 0 to 45000
- output_grad: float32 [16384, 5120], P('ctx', 'tp'), may hold values from -6 to 6
Outputs:
- input_grad: float32 [16384, 5120], P('ctx', 'tp')
- b_grad: float32 [16384, 128], P(('ctx', 'tp'))
- c_grad: float32 [16384, 128], P(('ctx', 'tp'))
- decay_grad: float32 [80, 16384], P('tp', 'ctx')
All inputs are finite; a program needn't handle non-finite values.
Results may differ from a plain program's by a relative error of at most 0.00029.
Values sent between devices are 32-bit elements; how exact they have to be, the bound alone decides.
No kernel may reach another device: no remote copies, remote signals or barrier semaphores. Data moves between devices by JAX's collectives and lax.ppermute only.
A program may use at most 64 MiB of HBM per device.

v0:
```python
import functools

import jax
import jax.numpy as jnp
from jax import lax
from jax.experimental import pallas as pl
from jax.experimental.pallas import tpu as pltpu
from jax.sharding import PartitionSpec as P

INTERPRET = False
F32 = jnp.float32
BF16 = jnp.bfloat16
CODE_UNIT = 2.0 ** (-16)
LANES = 128
MASKED = -1e30
GRANT = 12 << 20
LEAD_GRANT = 60 * 1024 * 1024

VMEM = pl.BlockSpec(memory_space=pltpu.VMEM)
SMEM = pl.BlockSpec(memory_space=pltpu.SMEM)
HBM = pl.BlockSpec(memory_space=pltpu.HBM)


def split(a):
    high = a.astype(BF16)
    return high, (a - high.astype(F32)).astype(BF16)


def nn(a, b):
    return lax.dot_general(a, b, (((1,), (0,)), ((), ())), preferred_element_type=F32)


def nt(a, b):
    return lax.dot_general(a, b, (((1,), (1,)), ((), ())), preferred_element_type=F32)


def three(product, a, b):
    return product(a[0], b[0]) + (product(a[0], b[1]) + product(a[1], b[0]))


def iota(shape, axis):
    return lax.broadcasted_iota(jnp.int32, shape, axis)


def spread(columns, pair, rows):
    first = columns[:, 2 * pair : 2 * pair + 1]
    second = columns[:, 2 * pair + 1 : 2 * pair + 2]
    return jnp.where(iota((rows, LANES), 1) < LANES // 2, first, second)


def block_state(scale, source_ref, side_ref, out_ref):
    rows, columns = source_ref.shape
    side = split(side_ref[...])
    for pair in range(columns // LANES):
        part = slice(pair * LANES, (pair + 1) * LANES)
        scaled = source_ref[:, part] * spread(scale, pair, rows)
        out_ref[part, :] = three(nn, split(scaled.T), side)


def halves(codes):
    return (codes >> 8).astype(F32).astype(BF16), (codes & 255).astype(F32).astype(BF16)


def decay_columns(high, low):
    rows = high.shape[1]
    lower = jnp.where(iota((rows, rows), 1) <= iota((rows, rows), 0), 1.0, 0.0).astype(BF16)
    return (256.0 * nt(lower, high) + nt(lower, low)) * -CODE_UNIT


def lead_kernel(
    late_ref, codes_hbm, x_hbm, dy_hbm, b_hbm, c_hbm, sent_ref, pairs_ref,
    codes_ref, source_ref, side_ref, sems,
):
    fetch_codes = pltpu.make_async_copy(codes_hbm, codes_ref, sems.at[0])
    fetch_codes.start()
    fetch_source = pltpu.make_async_copy(x_hbm, source_ref, sems.at[1])
    fetch_side = pltpu.make_async_copy(b_hbm, side_ref, sems.at[2])

    @pl.when(late_ref[0] == 1)
    def _():
        pltpu.make_async_copy(dy_hbm, source_ref, sems.at[1]).start()
        pltpu.make_async_copy(c_hbm, side_ref, sems.at[2]).start()

    @pl.when(late_ref[0] == 0)
    def _():
        fetch_source.start()
        fetch_side.start()

    fetch_codes.wait()
    codes = codes_ref[...]
    heads, rows = codes.shape
    high, low = halves(codes)
    columns = decay_columns(high, low)
    upper = jnp.where(iota((rows, rows), 0) <= iota((rows, rows), 1), 1.0, 0.0).astype(BF16)
    within = (256.0 * nn(high, upper) + nn(low, upper)) * -CODE_UNIT
    pairs_ref[...] = jnp.zeros_like(pairs_ref)
    for pair in range(heads // 2):
        pairs_ref[pair, 0:2, :] = within[2 * pair : 2 * pair + 2, :]
    final = columns[rows - 1 : rows, :]
    decay = jnp.exp(final)
    lane = iota((8, LANES), 1)
    line = jnp.zeros((8, LANES), F32)
    for head in range(heads):
        line = jnp.where(lane == head, decay[:, head : head + 1], line)
    sent_ref[source_ref.shape[1] :, :] = line
    scale = jnp.exp(jnp.where(late_ref[0] == 1, columns, final - columns))
    fetch_side.wait()
    fetch_source.wait()
    block_state(scale, source_ref, side_ref, sent_ref)


def own_kernel(late_ref, codes_ref, x_ref, dy_ref, b_ref, c_ref, own_ref):
    columns = decay_columns(*halves(codes_ref[...]))
    rows = columns.shape[0]

    @pl.when(late_ref[0] == 0)
    def _():
        block_state(jnp.exp(columns), dy_ref, c_ref, own_ref)

    @pl.when(late_ref[0] == 1)
    def _():
        block_state(jnp.exp(columns[rows - 1 : rows, :] - columns), x_ref, b_ref, own_ref)


def chip_kernel(heads, own_ref, sent_ref, got_ref, slab_hbm, total_ref, slab_ref, sems):
    height = own_ref.shape[0]
    width = height // heads
    chips, slab, lanes = slab_ref.shape
    per = height // chips
    mine = sent_ref[height : height + 1, :]
    theirs = got_ref[height : height + 1, :]
    for head in range(heads):
        part = slice(head * width, (head + 1) * width)
        total_ref[part, :] = own_ref[part, :] + mine[:, head : head + 1] * got_ref[part, :]
    both = mine * theirs
    lane = iota((slab - per, lanes), 1)
    line = iota((slab - per, lanes), 0)
    copies = []
    batch = chips // sems.shape[0]
    for chip in range(chips):
        slab_ref[chip, 0:per, :] = total_ref[chip * per : (chip + 1) * per, :]
        extra = jnp.zeros((slab - per, lanes), F32)
        for head in range(heads):
            low = max(head * width - chip * per, 0)
            high = min((head + 1) * width - chip * per, per)
            if low < high:
                here = (lane >= low) & (lane < high) & (line == 0)
                extra = jnp.where(here, both[:, head : head + 1], extra)
        slab_ref[chip, per:slab, :] = extra
        if (chip + 1) % batch == 0:
            part = pl.ds(chip + 1 - batch, batch)
            copies.append(pltpu.make_async_copy(slab_ref.at[part], slab_hbm.at[part], sems.at[len(copies)]))
            copies[-1].start()
    for copy in copies:
        copy.wait()


def scan_kernel(per, late_ref, got_ref, out_ref):
    chips, slab, lanes = got_ref.shape
    diagonal = iota((slab, lanes), 0) == iota((slab, lanes), 1)

    def run(order):
        carried = jnp.zeros((slab, lanes), F32)
        for chip in order:
            factor = jnp.sum(jnp.where(diagonal, got_ref[chip, per : per + 1, :], 0.0), axis=1, keepdims=True)
            for i in range(per // 4):
                out_ref[chip, i] = carried[4 * i : 4 * i + 4, :]
            carried = factor * carried + got_ref[chip]

    @pl.when(late_ref[0] == 1)
    def _():
        run(range(chips))

    @pl.when(late_ref[0] == 0)
    def _():
        run(range(chips - 1, -1, -1))


def unpack(slab_ref, out_ref):
    chips, pieces, tall, _ = slab_ref.shape
    for chip in range(chips):
        for i in range(pieces):
            at = (chip * pieces + i) * tall
            out_ref[at : at + tall, :] = slab_ref[chip, i]


def block_kernel(
    pairs_ref, x_ref, dy_ref, b_ref, c_ref,
    xs_high, xs_low, dys_high, dys_low, dx_ref, pair_ref, db_ref, dc_ref,
    scores_ref, grads_ref,
):
    step = pl.program_id(0)
    rows = x_ref.shape[0]
    half = rows // 2

    @pl.when(step == 0)
    def _():
        scores_ref[...] = three(nt, split(b_ref[...]), split(c_ref[...]))
        grads_ref[...] = jnp.zeros_like(grads_ref)

    lines = pairs_ref[0]
    columns = lines.T
    x = x_ref[...]
    dy = dy_ref[...]
    xs = split(x * spread(jnp.exp(lines.T[rows - 1 : rows, :] - columns), 0, rows))
    dys = split(dy * spread(jnp.exp(columns), 0, rows))
    xs_high[...], xs_low[...] = xs
    dys_high[...], dys_low[...] = dys
    x_high, x_low = split(x)
    left = iota((rows, LANES), 1) < LANES // 2
    lane = iota((rows, LANES), 1)
    sent = jnp.zeros((rows, LANES), F32)
    received = []
    totals = [0.0, 0.0]
    for i in range(2):
        masked = split(jnp.where(left if i == 0 else ~left, dy, 0.0))
        source_sums = []
        target_sum = None
        for b, start in enumerate((0, half)):
            part = slice(start, start + half)
            target = tuple(m[start:, :] for m in masked)
            products = three(nt, (x_high[part], x_low[part]), target)
            gap = lines[i : i + 1, start:] - columns[part, i : i + 1]
            shape = (half, rows - start)
            decays = jnp.exp(jnp.where(iota(shape, 1) >= iota(shape, 0), gap, MASKED))
            scores = scores_ref[part, start:]
            weighted = decays * products
            grads_ref[part, start:] += weighted
            terms = weighted * scores
            source_sums.append(jnp.sum(terms, axis=1, keepdims=True))
            sums = jnp.sum(terms, axis=0, keepdims=True)
            if b == 0:
                target_sum = sums
            else:
                target_sum = jnp.concatenate([target_sum[:, :half], target_sum[:, half:] + sums], axis=1)
            totals[b] += three(nn, split(decays * scores), target)
        sent = jnp.where(lane == i, jnp.concatenate(source_sums, axis=0), sent)
        received.append(target_sum)
    dx_ref[0:half, :] = totals[0]
    dx_ref[half:, :] = totals[1]
    line = iota((8, rows), 0)
    gained = jnp.where(line == 0, received[0], jnp.where(line == 1, received[1], 0.0))
    pair_ref[0] = gained - sent.T[0:8, :]

    @pl.when(step == pl.num_programs(0) - 1)
    def _():
        grads = grads_ref[...]
        db_ref[...] = three(nn, split(grads), split(c_ref[...]))
        dc_ref[...] = three(nn, split(grads.T), split(b_ref[...]))


def through_kernel(
    heads, late_ref, back_ref, got_ref, xs_high, xs_low, dys_high, dys_low, through_hbm, far_ref, through_ref, sem
):
    height = through_ref.shape[0]
    width = height // heads
    unpack(back_ref, through_ref)
    decay = got_ref[height : height + 1, :]
    for head in range(heads):
        part = slice(head * width, (head + 1) * width)
        through_ref[part, :] = decay[:, head : head + 1] * through_ref[part, :] + got_ref[part, :]
    copy = pltpu.make_async_copy(through_ref, through_hbm, sem)
    copy.start()

    @pl.when(late_ref[0] == 1)
    def _():
        far_ref[...] = three(nn, (dys_high[...], dys_low[...]), split(through_ref[...]))

    @pl.when(late_ref[0] == 0)
    def _():
        far_ref[...] = three(nn, (xs_high[...], xs_low[...]), split(through_ref[...]))

    copy.wait()


def rows_kernel(
    late_ref, theirs_ref, xs_high, xs_low, dys_high, dys_low, far_ref, db_ref, dc_ref, out_hbm, state_ref, out_ref, sems
):
    unpack(theirs_ref, state_ref)
    parts, tall, _ = out_ref.shape
    tall = tall // 2

    def send(which, value):
        side = slice(which * tall, (which + 1) * tall)
        for part in range(parts):
            out_ref[part, side, :] = value[part * tall : (part + 1) * tall, :]
        copy = pltpu.make_async_copy(
            out_ref.at[:, pl.ds(which * tall, tall), :], out_hbm.at[:, pl.ds(which * tall, tall), :], sems.at[which]
        )
        copy.start()
        return copy

    @pl.when(late_ref[0] == 1)
    def _():
        first = send(1, dc_ref[...] + far_ref[...])
        second = send(0, db_ref[...] + three(nn, (xs_high[...], xs_low[...]), split(state_ref[...])))
        first.wait()
        second.wait()

    @pl.when(late_ref[0] == 0)
    def _():
        first = send(0, db_ref[...] + far_ref[...])
        second = send(1, dc_ref[...] + three(nn, (dys_high[...], dys_low[...]), split(state_ref[...])))
        first.wait()
        second.wait()


def last_kernel(
    late_ref, pairs_ref, through_ref, slab_ref, x_ref, dy_ref, b_ref, c_ref, near_ref, pair_ref,
    dx_hbm, out_ref, theirs_ref, dx_ref, sems,
):
    rows, height = x_ref.shape
    pairs = height // LANES
    half = LANES // 2
    late = late_ref[0] == 1
    unpack(slab_ref, theirs_ref)
    b, c = split(b_ref[...]), split(c_ref[...])
    picks = jnp.where((iota((8, LANES), 1) < half) == (iota((8, LANES), 0) == 0), 1.0, 0.0)
    picks = jnp.where(iota((8, LANES), 0) < 2, picks, 0.0).astype(BF16)
    first, second = iota((rows, rows), 0), iota((rows, rows), 1)
    earlier = jnp.where(first < second, 1.0, 0.0).astype(BF16)
    line = iota((8, rows), 0)
    copies = []
    left_lines, through_lines, enter_lines = [], [], []
    for pair in range(pairs):
        part = slice(pair * LANES, (pair + 1) * LANES)
        lines = pairs_ref[pair]
        columns = lines.T
        mine, other = through_ref[part, :], theirs_ref[part, :]
        start = jnp.where(late, mine, other)
        end = jnp.where(late, other, mine)
        entered = three(nt, c, split(start)) * spread(jnp.exp(columns), 0, rows)
        leaving = three(nt, b, split(end)) * spread(jnp.exp(columns[rows - 1 : rows, :] - columns), 0, rows)
        dx_ref[:, part] = near_ref[:, part] + leaving
        copies.append(pltpu.make_async_copy(dx_ref.at[:, part], dx_hbm.at[:, part], sems.at[pair]))
        copies[-1].start()
        enter = split(dy_ref[:, part] * entered)
        leave = split(x_ref[:, part] * leaving)
        enter_lines.append(nt(picks, enter[0]) + nt(picks, enter[1]))
        left_lines.append(nt(picks, leave[0]) + nt(picks, leave[1]))
        across = jnp.sum(mine * other, axis=1, keepdims=True)
        passed = [jnp.sum(across[i * half : (i + 1) * half], axis=0, keepdims=True) for i in range(2)]
        decay = jnp.exp(lines[:, rows - 1 : rows])
        through_lines.append(decay * jnp.where(line == 0, passed[0], jnp.where(line == 1, passed[1], 0.0)))
    later = jnp.where(first >= second, 1.0, 0.0).astype(BF16)

    def exact(lines, ones):
        a = jnp.concatenate(lines, axis=0)
        high, low = split(a)
        rest = (a - high.astype(F32) - low.astype(F32)).astype(BF16)
        return nn(high, ones) + (nn(low, ones) + nn(rest, ones))

    gained = exact([pair_ref[p] + enter_lines[p] for p in range(pairs)], later) + exact(left_lines, earlier)
    total = gained + jnp.concatenate(through_lines, axis=0)
    for pair in range(pairs):
        out_ref[2 * pair : 2 * pair + 2, :] = total[8 * pair : 8 * pair + 2, :]
    for copy in copies:
        copy.wait()


def call(kernel, name, in_specs, out_shape, flops, moved, grant=GRANT, **rest):
    return pl.pallas_call(
        kernel,
        name=name,
        in_specs=in_specs,
        out_shape=out_shape,
        cost_estimate=pl.CostEstimate(flops=flops, bytes_accessed=moved, transcendentals=0),
        interpret=INTERPRET,
        compiler_params=pltpu.CompilerParams(vmem_limit_bytes=grant),
        **rest,
    )


def shape(*dims, dtype=F32):
    return jax.ShapeDtypeStruct(dims, dtype)


def stored(*dims):
    return shape(*dims) if INTERPRET else pltpu.HBM(dims, F32)


def swap_cores(value, count):
    return lax.ppermute(value, "ctx", [(i, i ^ 1) for i in range(count)])


def exchange(value, count):
    groups = [[2 * k + c for k in range(count // 2)] for c in range(2)]
    return lax.all_to_all(value, "ctx", 0, 0, axis_index_groups=groups, tiled=True)


def per_device(inputs, state_input, state_output, decay_codes, output_grad):
    count = lax.axis_size("ctx")
    parts = lax.axis_size("tp")
    heads, rows = decay_codes.shape
    height = inputs.shape[1]
    state = state_input.shape[1]
    pairs = height // LANES
    chips = count // 2
    per = height // chips
    slab = -(-(per + 1) // 8) * 8
    late = (lax.axis_index("ctx") & 1).astype(jnp.int32).reshape(1)
    operands = (inputs, output_grad, state_input, state_output)
    wide = rows * height * 4
    square = 2 * rows * height * state * 3

    sent, lines = call(
        lead_kernel, "lead", [SMEM] + [HBM] * 5, (shape(height + 8, state), shape(pairs, 8, rows)),
        square, 2 * wide, out_specs=(VMEM,) * 2, grant=LEAD_GRANT,
        scratch_shapes=[
            pltpu.VMEM((heads, rows), jnp.int32), pltpu.VMEM((rows, height), F32), pltpu.VMEM((rows, state), F32),
            pltpu.SemaphoreType.DMA((3,)),
        ],
    )(late, decay_codes, *operands)
    got = swap_cores(sent, count)
    own = call(
        own_kernel, "own", [SMEM] + [VMEM] * 5, shape(height, state), square, 3 * wide, out_specs=VMEM,
    )(late, decay_codes, *operands)
    total = call(
        functools.partial(chip_kernel, heads), "chip", [VMEM] * 3, stored(chips, slab, state),
        height * state, wide, out_specs=HBM,
        scratch_shapes=[
            pltpu.VMEM((height, state), F32), pltpu.VMEM((chips, slab, state), F32), pltpu.SemaphoreType.DMA((4,)),
        ],
    )(own, sent, got)
    slices = exchange(total, count)

    tile = pl.BlockSpec((rows, LANES), lambda i: (0, i))
    whole = pl.BlockSpec((rows, state), lambda i: (0, 0))
    line = pl.BlockSpec((1, 8, rows), lambda i: (i, 0, 0))
    *scaled, near, pair_sums, db, dc = call(
        block_kernel, "block", [line, tile, tile, whole, whole],
        (*[shape(rows, height, dtype=BF16)] * 4,
         stored(rows, height), stored(pairs, 8, rows), stored(rows, state), stored(rows, state)),
        8 * square, 6 * wide, grid=(pairs,),
        out_specs=[tile] * 5 + [line, whole, whole],
        scratch_shapes=[pltpu.VMEM((rows, rows), F32)] * 2,
    )(lines, *operands)
    slices, *near_parts = lax.optimization_barrier((slices, *scaled, near, pair_sums, db, dc))
    *scaled, near, pair_sums, db, dc = near_parts
    before = call(
        functools.partial(scan_kernel, per), "scan", [SMEM, VMEM], shape(chips, per // 4, 4, state),
        height * state, wide, out_specs=VMEM,
    )(late, slices)
    back = exchange(before, count)
    theirs = swap_cores(back, count)
    through, far = call(
        functools.partial(through_kernel, heads), "through", [SMEM] + [VMEM] * 6,
        (stored(height, state), shape(rows, state)), square, 3 * wide, out_specs=(HBM, VMEM),
        scratch_shapes=[pltpu.VMEM((height, state), F32), pltpu.SemaphoreType.DMA],
    )(late, back, got, *scaled)
    packed = call(
        rows_kernel, "rows", [SMEM] + [VMEM] * 8, stored(parts, 2 * rows // parts, state),
        square, 3 * wide, out_specs=HBM,
        scratch_shapes=[
            pltpu.VMEM((height, state), F32), pltpu.VMEM((parts, 2 * rows // parts, state), F32),
            pltpu.SemaphoreType.DMA((2,)),
        ],
    )(late, theirs, *scaled, far, db, dc)
    summed = jnp.sum(lax.all_to_all(packed, "tp", 0, 0, tiled=True), axis=0)

    input_grad, decay_grad = call(
        last_kernel, "last", [SMEM] + [VMEM] * 9, (shape(rows, height), shape(heads, rows)),
        2 * square, 6 * wide, out_specs=(HBM, VMEM),
        scratch_shapes=[
            pltpu.VMEM((height, state), F32), pltpu.VMEM((rows, height), F32), pltpu.SemaphoreType.DMA((pairs,)),
        ],
    )(late, lines, through, theirs, *operands, near, pair_sums)
    tall = rows // parts
    return (input_grad, summed[:tall], summed[tall:], decay_grad)


def solution(mesh):
    placed = (P("ctx", "tp"), P("ctx", None), P("ctx", None), P("tp", "ctx"), P("ctx", "tp"))
    return jax.shard_map(
        per_device,
        mesh=mesh,
        in_specs=placed,
        out_specs=(P("ctx", "tp"), P(("ctx", "tp"), None), P(("ctx", "tp"), None), P("tp", "ctx")),
        check_vma=False,
    )
```

profile of v0, /device:TPU:73, one launch (start us, length us, event | category | flops | bytes accessed | tf_op | source)
XLA Modules:
  0.0 83.5 jit_solution(17499300349854188739)
XLA Ops:
  0.6 0.0 copy-start
  0.6 0.0 copy-start.1
  0.7 0.0 copy-start.2
  0.7 0.0 copy-start.3
  0.7 0.0 copy-start.11
  0.7 2.9 %lead.1 = (f32[648,128]{1,0:T(8,128)}, f32[5,8,256]{2,1,0:T(8,128)}) custom-call(s32[1]{0:T(128)} %bitcast.late_ref, s32[10,256]{1,0:T(8,128)} %codes_ref.1, f32[256,640]{1,0:T(8,128)} %x_ref.5, f32[256,640]{1,0:T(8,128)} %dy_ref.5, f32[256,128]{1,0:T(8,128)} %b_ref.5, f32[256,128]{1,0:T(8,128)} %c_ref.5), custom_call_target="tpu_custom_call" | custom-call | flops 125829120 | bytes 1310720 | tf_op jit(solution)/shard_map/lead/pallas_call | solution.py:406
  3.6 0.0 copy-start.7
  3.6 2.7 %collective-permute-start = (f32[648,128]{1,0:T(8,128)}, f32[648,128]{1,0:T(8,128)S(1)}, u32[]{:S(2)}, u32[]{:S(2)}) collective-permute-start(f32[648,128]{1,0:T(8,128)} %get-tuple-element.28.sent_ref), channel_id=1, source_target_pairs={{0,8},{8,0},{16,24},{24,16},{32,40},{40,32},{48,56},{56,48},{64,72... | collective-permute-start | bytes 995336 | tf_op jit(solution)/shard_map/ppermute | solution.py:383
  6.4 0.0 copy-done
  6.4 1.2 %own.1.own_ref = f32[640,128]{1,0:T(8,128)S(1)} custom-call(s32[1]{0:T(128)} %bitcast.late_ref, s32[10,256]{1,0:T(8,128)S(1)} %copy-done.11, f32[256,640]{1,0:T(8,128)S(1)} %copy-done, f32[256,640]{1,0:T(8,128)S(1)} %copy-done.1, f32[256,128]{1,0:T(8,128)S(1)} %copy-done.2, f32[256,128]{1,0:T(8,128)S(1)} %copy-done.3), custom_call_target="tpu_custom_call" | custom-call | flops 125829120 | bytes 1966080 | tf_op jit(solution)/shard_map/own/pallas_call | solution.py:415
  7.6 0.2 collective-permute-done.got_ref
  7.8 0.9 %chip.1 = f32[32,24,128]{2,1,0:T(8,128)} custom-call(f32[640,128]{1,0:T(8,128)S(1)} %own.1.own_ref, f32[648,128]{1,0:T(8,128)S(1)} %copy-done.7, f32[648,128]{1,0:T(8,128)S(1)} %collective-permute-done.got_ref), custom_call_target="tpu_custom_call" | custom-call | flops 81920 | bytes 655360 | tf_op jit(solution)/shard_map/chip/pallas_call | solution.py:418
  8.7 0.0 copy-start.12
  8.8 11.7 %all-to-all-start = ((f32[32,24,128]{2,1,0:T(8,128)}), f32[32,24,128]{2,1,0:T(8,128)S(1)}, u32[]{:S(2)}, u32[]{:S(2)}) async-start(f32[32,24,128]{2,1,0:T(8,128)} %chip.1), calls=%async_computation | async-start | bytes 786432 | tf_op jit(solution)/shard_map/all_to_all | solution.py:388
  20.5 0.0 copy-start.4
  20.5 0.9 %copy-done.4 = f32[256,128]{1,0:T(8,128)S(1)} copy-done((f32[256,128]{1,0:T(8,128)S(1)}, f32[256,128]{1,0:T(8,128)}, u32[]{:S(2)}) %copy-start.4) | copy-done | bytes 131096
  21.4 7.3 %block.1 = (bf16[256,640]{1,0:T(8,128)(2,1)S(1)}, bf16[256,640]{1,0:T(8,128)(2,1)S(1)}, bf16[256,640]{1,0:T(8,128)(2,1)S(1)}, bf16[256,640]{1,0:T(8,128)(2,1)S(1...) custom-call(f32[5,8,256]{2,1,0:T(8,128)S(1)} %copy-done.12, ...), custom_call_target="tpu_custom_call" | custom-call | flops 1006632960 | bytes 3932160 | tf_op jit(solution)/shard_map/block/pallas_call | solution.py:430
  28.6 5.2 %all-to-all-done.got_ref = f32[32,24,128]{2,1,0:T(8,128)S(1)} async-done(((f32[32,24,128]{2,1,0:T(8,128)}), f32[32,24,128]{2,1,0:T(8,128)S(1)}, u32[]{:S(2)}, u32[]{:S(2)}) %all-to-all-start) | async-done | bytes 393248 | tf_op jit(solution)/shard_map/all_to_all | solution.py:388
  33.9 0.2 scan.1
  34.1 17.9 %all_to_all.15.back_ref = f32[32,5,4,128]{3,2,1,0:T(4,128)S(1)} all-to-all(f32[32,5,4,128]{3,2,1,0:T(4,128)S(1)} %scan.1), channel_id=1, replica_groups={{0,16,32,48,64,80,96,112,128,144,160,176,192,208,224,240,256,272,288,30..., dimensions={0} | all-to-all | bytes 655360 | tf_op jit(solution)/shard_map/all_to_all | solution.py:388
  52.0 4.1 %collective-permute-start.1 = (f32[32,5,4,128]{3,2,1,0:T(4,128)S(1)}, f32[32,5,4,128]{3,2,1,0:T(4,128)S(1)}, u32[]{:S(2)}, u32[]{:S(2)}) collective-permute-start(f32[32,5,4,128]{3,2,1,0:T(4,128)S(1)} %all_to_all.15.back_ref), channel_id=1, source_target_pairs={{0,8},{8,0},{16,24},{24,16},{32,40},{40,32},{48,56},{56,48},{64,72... | collective-permute-start | bytes 983048 | tf_op jit(solution)/shard_map/ppermute | solution.py:383
  56.2 0.9 %through.1 = (f32[640,128]{1,0:T(8,128)}, f32[256,128]{1,0:T(8,128)S(1)}) custom-call(s32[1]{0:T(128)} %bitcast.late_ref, f32[32,5,4,128]{3,2,1,0:T(4,128)S(1)} %all_to_all.15.back_ref, f32[648,128]{1,0:T(8,128)S(1)} %collective-permute-done.got_ref, bf16[256,640]{1,0:T(8,128)(2,1)S(1)} %get-tuple-element.38.xs_high, ...), custom_call_target="tpu_custom_call" | custom-call | flops 125829120 | bytes 1966080 | tf_op jit(solution)/shard_map/through/pallas_call | solution.py:446
  57.0 0.4 collective-permute-done.1.slab_ref.theirs_ref
  57.4 0.0 copy-done.9
  57.4 1.1 %rows.1 = f32[8,64,128]{2,1,0:T(8,128)} custom-call(s32[1]{0:T(128)} %bitcast.late_ref, f32[32,5,4,128]{3,2,1,0:T(4,128)S(1)} %collective-permute-done.1.slab_ref.theirs_ref, bf16[256,640]{1,0:T(8,128)(2,1)S(1)} %get-tuple-element.38.xs_high, bf16[256,640]{1,0:T(8,128)(2,1)S(1)} %get-tuple-element.39.xs_low, ...), custom_call_target="tpu_custom_call" | custom-call | flops 125829120 | bytes 1966080 | tf_op jit(solution)/shard_map/rows/pallas_call | solution.py:451
  58.5 0.0 copy-start.5
  58.6 9.9 %all-to-all-start.2 = ((f32[8,64,128]{2,1,0:T(8,128)}), f32[8,64,128]{2,1,0:T(8,128)S(1)}, u32[]{:S(2)}, u32[]{:S(2)}) async-start(f32[8,64,128]{2,1,0:T(8,128)} %rows.1), calls=%async_computation.2 | async-start | bytes 524288 | tf_op jit(solution)/shard_map/all_to_all | solution.py:459
  68.5 0.0 copy-start.6
  68.5 1.1 %copy-done.6 = f32[256,640]{1,0:T(8,128)S(1)} copy-done((f32[256,640]{1,0:T(8,128)S(1)}, f32[256,640]{1,0:T(8,128)}, u32[]{:S(2)}) %copy-start.6) | copy-done | bytes 655384
  69.6 3.2 %last.1 = (f32[256,640]{1,0:T(8,128)}, f32[10,256]{1,0:T(8,128)}) custom-call(s32[1]{0:T(128)} %bitcast.late_ref, f32[5,8,256]{2,1,0:T(8,128)S(1)} %copy-done.12, f32[640,128]{1,0:T(8,128)S(1)} %copy-done.8, f32[32,5,4,128]{3,2,1,0:T(4,128)S(1)} %collective-permute-done.1.slab_ref.theirs_ref, f32[256,640]{1,0:T(8,128)S(1)} %copy-done, ...), custom_call_target="tpu_custom_call" | custom-call | flops 251658240 | bytes 3932160 | tf_op jit(solution)/shard_map/last/pallas_call | solution.py:461
  72.8 10.1 %all-to-all-done.2 = f32[8,64,128]{2,1,0:T(8,128)S(1)} async-done(((f32[8,64,128]{2,1,0:T(8,128)}), f32[8,64,128]{2,1,0:T(8,128)S(1)}, u32[]{:S(2)}, u32[]{:S(2)}) %all-to-all-start.2) | async-done | bytes 262176 | tf_op jit(solution)/shard_map/all_to_all | solution.py:459
  82.9 0.6 fusion
  (15 shorter events, 0.0 us)
Async XLA Ops:
  0.6 5.7 %copy-start = (f32[256,640]{1,0:T(8,128)S(1)}, f32[256,640]{1,0:T(8,128)}, u32[]{:S(2)}) copy-start(f32[256,640]{1,0:T(8,128)} %x_ref.5) | copy-start | bytes 1966084
  0.6 5.7 %copy-start.1 = (f32[256,640]{1,0:T(8,128)S(1)}, f32[256,640]{1,0:T(8,128)}, u32[]{:S(2)}) copy-start(f32[256,640]{1,0:T(8,128)} %dy_ref.5) | copy-start | bytes 1966084
  0.7 5.7 %copy-start.2 = (f32[256,128]{1,0:T(8,128)S(1)}, f32[256,128]{1,0:T(8,128)}, u32[]{:S(2)}) copy-start(f32[256,128]{1,0:T(8,128)} %b_ref.5) | copy-start | bytes 393220
  0.7 5.7 %copy-start.3 = (f32[256,128]{1,0:T(8,128)S(1)}, f32[256,128]{1,0:T(8,128)}, u32[]{:S(2)}) copy-start(f32[256,128]{1,0:T(8,128)} %c_ref.5) | copy-start | bytes 393220
  0.7 5.7 %copy-start.11 = (s32[10,256]{1,0:T(8,128)S(1)}, s32[10,256]{1,0:T(8,128)}, u32[]{:S(2)}) copy-start(s32[10,256]{1,0:T(8,128)} %codes_ref.1) | copy-start | bytes 30724
  3.6 4.2 %copy-start.7 = (f32[648,128]{1,0:T(8,128)S(1)}, f32[648,128]{1,0:T(8,128)}, u32[]{:S(2)}) copy-start(f32[648,128]{1,0:T(8,128)} %get-tuple-element.28.sent_ref) | copy-start | bytes 995332
  3.6 4.2 %collective-permute-start = (f32[648,128]{1,0:T(8,128)}, f32[648,128]{1,0:T(8,128)S(1)}, u32[]{:S(2)}, u32[]{:S(2)}) collective-permute-start(f32[648,128]{1,0:T(8,128)} %get-tuple-element.28.sent_ref), channel_id=1, source_target_pairs={{0,8},{8,0},{16,24},{24,16},{32,40},{40,32},{48,56},{56,48},{64,72... | collective-permute-start | bytes 995336 | tf_op jit(solution)/shard_map/ppermute | solution.py:383
  8.7 11.7 %copy-start.12 = (f32[5,8,256]{2,1,0:T(8,128)S(1)}, f32[5,8,256]{2,1,0:T(8,128)}, u32[]{:S(2)}) copy-start(f32[5,8,256]{2,1,0:T(8,128)} %get-tuple-element.27.pairs_ref) | copy-start | bytes 122884
  8.8 25.1 %all-to-all-start = ((f32[32,24,128]{2,1,0:T(8,128)}), f32[32,24,128]{2,1,0:T(8,128)S(1)}, u32[]{:S(2)}, u32[]{:S(2)}) async-start(f32[32,24,128]{2,1,0:T(8,128)} %chip.1), calls=%async_computation | async-start | bytes 786432 | tf_op jit(solution)/shard_map/all_to_all | solution.py:388
  20.5 0.9 %copy-start.4 = (f32[256,128]{1,0:T(8,128)S(1)}, f32[256,128]{1,0:T(8,128)}, u32[]{:S(2)}) copy-start(f32[256,128]{1,0:T(8,128)} %c_ref.5) | copy-start | bytes 393220
  52.0 5.4 %copy-start.9 = (f32[256,128]{1,0:T(8,128)S(1)}, f32[256,128]{1,0:T(8,128)}, u32[]{:S(2)}) copy-start(f32[256,128]{1,0:T(8,128)} %get-tuple-element.47.db_ref) | copy-start | bytes 393220
  52.0 5.4 %copy-start.10 = (f32[256,128]{1,0:T(8,128)S(1)}, f32[256,128]{1,0:T(8,128)}, u32[]{:S(2)}) copy-start(f32[256,128]{1,0:T(8,128)} %get-tuple-element.48.dc_ref) | copy-start | bytes 393220
  52.0 5.4 %collective-permute-start.1 = (f32[32,5,4,128]{3,2,1,0:T(4,128)S(1)}, f32[32,5,4,128]{3,2,1,0:T(4,128)S(1)}, u32[]{:S(2)}, u32[]{:S(2)}) collective-permute-start(f32[32,5,4,128]{3,2,1,0:T(4,128)S(1)} %all_to_all.15.back_ref), channel_id=1, source_target_pairs={{0,8},{8,0},{16,24},{24,16},{32,40},{40,32},{48,56},{56,48},{64,72... | collective-permute-start | bytes 983048 | tf_op jit(solution)/shard_map/ppermute | solution.py:383
  58.5 9.9 %copy-start.5 = (f32[256,128]{1,0:T(8,128)S(1)}, f32[256,128]{1,0:T(8,128)}, u32[]{:S(2)}) copy-start(f32[256,128]{1,0:T(8,128)} %c_ref.5) | copy-start | bytes 393220
  58.5 9.9 %copy-start.8 = (f32[640,128]{1,0:T(8,128)S(1)}, f32[640,128]{1,0:T(8,128)}, u32[]{:S(2)}) copy-start(f32[640,128]{1,0:T(8,128)} %get-tuple-element.42.through_ref) | copy-start | bytes 983044
  58.5 9.9 %copy-start.13 = (f32[5,8,256]{2,1,0:T(8,128)S(1)}, f32[5,8,256]{2,1,0:T(8,128)}, u32[]{:S(2)}) copy-start(f32[5,8,256]{2,1,0:T(8,128)} %get-tuple-element.44.pair_ref) | copy-start | bytes 122884
  58.6 24.3 %all-to-all-start.2 = ((f32[8,64,128]{2,1,0:T(8,128)}), f32[8,64,128]{2,1,0:T(8,128)S(1)}, u32[]{:S(2)}, u32[]{:S(2)}) async-start(f32[8,64,128]{2,1,0:T(8,128)} %rows.1), calls=%async_computation.2 | async-start | bytes 524288 | tf_op jit(solution)/shard_map/all_to_all | solution.py:459
  68.5 1.1 %copy-start.6 = (f32[256,640]{1,0:T(8,128)S(1)}, f32[256,640]{1,0:T(8,128)}, u32[]{:S(2)}) copy-start(f32[256,640]{1,0:T(8,128)} %get-tuple-element.43.near_ref) | copy-start | bytes 1966084
where the time goes:
time: 84 us; the launch traced here: 83.5 us
  starting transfers between devices  28.4 us (34%)
  blocking collectives  17.9 us (21%)
  Pallas kernels  17.7 us (21%)
  waiting for transfers between devices  15.9 us (19%)
  local copies, waits for them, and re-layouts  2.65 us (3%)
  between operations  0.89 us (1%)
    all_to_all x1, blocking collectives, exchange(): lax.all_to_all(value, 'ctx', 0, 0, axis_index_groups=groups, tiled=True)  17.9 us
    all_to_all x1, starting transfers between devices, exchange(): lax.all_to_all(value, 'ctx', 0, 0, axis_index_groups=groups, tiled=True)  11.7 us
    all_to_all x1, waiting for transfers between devices, per_device(): summed = jnp.sum(lax.all_to_all(packed, 'tp', 0, 0, tiled=True), axis=0)  10.1 us
    all_to_all x1, starting transfers between devices, per_device(): summed = jnp.sum(lax.all_to_all(packed, 'tp', 0, 0, tiled=True), axis=0)  9.91 us
    pallas_call x1, Pallas kernels, per_device(): call(block_kernel, 'block', [line, tile, tile, whole, whole], (*[shape(ro...  7.28 us
    ppermute x2, starting transfers between devices, swap_cores(): return lax.ppermute(value, 'ctx', [(i, i ^ 1) for i in range(count)])  6.86 us
    all_to_all x1, waiting for transfers between devices, exchange(): lax.all_to_all(value, 'ctx', 0, 0, axis_index_groups=groups, tiled=True)  5.25 us
    pallas_call x1, Pallas kernels, per_device(): call(last_kernel, 'last', [SMEM] + [VMEM] * 9, (shape(rows, height), shap...  3.2 us
  transfers between devices with their start and end apart: 4, of which 4 were waited for; matrix products, arithmetic and copies ran while one was open for 0% of the time, Pallas kernels for 15%

commit v1 on v0

--- a/solution.py
+++ b/solution.py
@@ -15,10 +15,18 @@
 MASKED = -1e30
 GRANT = 12 << 20
 LEAD_GRANT = 60 * 1024 * 1024
+OUT_FIRST = 20
+BACK_FIRST = 20
+SUM_FIRST = 3
 
 VMEM = pl.BlockSpec(memory_space=pltpu.VMEM)
 SMEM = pl.BlockSpec(memory_space=pltpu.SMEM)
 HBM = pl.BlockSpec(memory_space=pltpu.HBM)
+
+
+def listed(members, first):
+    first = first % members
+    return [first] + [k for k in range(members) if k != first]
 
 
 def split(a):
@@ -159,13 +167,16 @@
     chips, slab, lanes = got_ref.shape
     diagonal = iota((slab, lanes), 0) == iota((slab, lanes), 1)
 
+    arrived, leaving = listed(chips, OUT_FIRST), listed(chips, BACK_FIRST)
+
     def run(order):
         carried = jnp.zeros((slab, lanes), F32)
         for chip in order:
-            factor = jnp.sum(jnp.where(diagonal, got_ref[chip, per : per + 1, :], 0.0), axis=1, keepdims=True)
+            at, to = arrived.index(chip), leaving.index(chip)
+            factor = jnp.sum(jnp.where(diagonal, got_ref[at, per : per + 1, :], 0.0), axis=1, keepdims=True)
             for i in range(per // 4):
-                out_ref[chip, i] = carried[4 * i : 4 * i + 4, :]
-            carried = factor * carried + got_ref[chip]
+                out_ref[to, i] = carried[4 * i : 4 * i + 4, :]
+            carried = factor * carried + got_ref[at]
 
     @pl.when(late_ref[0] == 1)
     def _():
@@ -178,10 +189,11 @@
 
 def unpack(slab_ref, out_ref):
     chips, pieces, tall, _ = slab_ref.shape
-    for chip in range(chips):
+    owned = listed(chips, OUT_FIRST)
+    for place, chip in enumerate(listed(chips, BACK_FIRST)):
         for i in range(pieces):
-            at = (chip * pieces + i) * tall
-            out_ref[at : at + tall, :] = slab_ref[chip, i]
+            at = (owned.index(chip) * pieces + i) * tall
+            out_ref[at : at + tall, :] = slab_ref[place, i]
 
 
 def block_kernel(
@@ -279,11 +291,12 @@
     unpack(theirs_ref, state_ref)
     parts, tall, _ = out_ref.shape
     tall = tall // 2
+    places = listed(parts, SUM_FIRST)
 
     def send(which, value):
         side = slice(which * tall, (which + 1) * tall)
         for part in range(parts):
-            out_ref[part, side, :] = value[part * tall : (part + 1) * tall, :]
+            out_ref[places.index(part), side, :] = value[part * tall : (part + 1) * tall, :]
         copy = pltpu.make_async_copy(
             out_ref.at[:, pl.ds(which * tall, tall), :], out_hbm.at[:, pl.ds(which * tall, tall), :], sems.at[which]
         )
@@ -383,8 +396,8 @@
     return lax.ppermute(value, "ctx", [(i, i ^ 1) for i in range(count)])
 
 
-def exchange(value, count):
-    groups = [[2 * k + c for k in range(count // 2)] for c in range(2)]
+def exchange(value, count, first):
+    groups = [[2 * k + c for k in listed(count // 2, first)] for c in range(2)]
     return lax.all_to_all(value, "ctx", 0, 0, axis_index_groups=groups, tiled=True)
 
 
@@ -422,7 +435,7 @@
             pltpu.VMEM((height, state), F32), pltpu.VMEM((chips, slab, state), F32), pltpu.SemaphoreType.DMA((4,)),
         ],
     )(own, sent, got)
-    slices = exchange(total, count)
+    slices = exchange(total, count, OUT_FIRST)
 
     tile = pl.BlockSpec((rows, LANES), lambda i: (0, i))
     whole = pl.BlockSpec((rows, state), lambda i: (0, 0))
@@ -441,7 +454,7 @@
         functools.partial(scan_kernel, per), "scan", [SMEM, VMEM], shape(chips, per // 4, 4, state),
         height * state, wide, out_specs=VMEM,
     )(late, slices)
-    back = exchange(before, count)
+    back = exchange(before, count, BACK_FIRST)
     theirs = swap_cores(back, count)
     through, far = call(
         functools.partial(through_kernel, heads), "through", [SMEM] + [VMEM] * 6,
@@ -456,7 +469,7 @@
             pltpu.SemaphoreType.DMA((2,)),
         ],
     )(late, theirs, *scaled, far, db, dc)
-    summed = jnp.sum(lax.all_to_all(packed, "tp", 0, 0, tiled=True), axis=0)
+    summed = jnp.sum(lax.all_to_all(packed, "tp", 0, 0, axis_index_groups=[listed(parts, SUM_FIRST)], tiled=True), axis=0)
 
     input_grad, decay_grad = call(
         last_kernel, "last", [SMEM] + [VMEM] * 9, (shape(rows, height), shape(heads, rows)),

time: 84 us -> 74.6 us (0.89)
  the two profiles are of different devices: /device:TPU:73 before, /device:TPU:64 now
where the time goes in v1:
time: 74.6 us; the launch traced here: 74.1 us
  starting transfers between devices  27.4 us (37%)
  Pallas kernels  17.7 us (24%)
  blocking collectives  17.3 us (23%)
  waiting for transfers between devices  8.12 us (11%)
  local copies, waits for them, and re-layouts  2.65 us (4%)
  between operations  0.88 us (1%)
    all_to_all x1, blocking collectives, exchange(): lax.all_to_all(value, 'ctx', 0, 0, axis_index_groups=groups, tiled=True)  17.3 us
    all_to_all x1, starting transfers between devices, exchange(): lax.all_to_all(value, 'ctx', 0, 0, axis_index_groups=groups, tiled=True)  12.7 us
    all_to_all x1, starting transfers between devices, per_device(): lax.all_to_all(packed, 'tp', 0, 0, axis_index_groups=[listed(parts, SUM_F...  10.6 us
    pallas_call x1, Pallas kernels, per_device(): call(block_kernel, 'block', [line, tile, tile, whole, whole], (*[shape(ro...  7.28 us
    all_to_all x1, waiting for transfers between devices, per_device(): lax.all_to_all(packed, 'tp', 0, 0, axis_index_groups=[listed(parts, SUM_F...  4.45 us
    ppermute x2, starting transfers between devices, swap_cores(): return lax.ppermute(value, 'ctx', [(i, i ^ 1) for i in range(count)])  4.09 us
    pallas_call x1, Pallas kernels, per_device(): call(last_kernel, 'last', [SMEM] + [VMEM] * 9, (shape(rows, height), shap...  3.2 us
    pallas_call x1, Pallas kernels, per_device(): call(lead_kernel, 'lead', [SMEM] + [HBM] * 5, (shape(height + 8, state),...  2.93 us
  transfers between devices with their start and end apart: 4, of which 4 were waited for; matrix products, arithmetic and copies ran while one was open for 0% of the time, Pallas kernels for 17%

profile of v1, /device:TPU:64, one launch (start us, length us, event | category | flops | bytes accessed | tf_op | source)
XLA Modules:
  0.0 74.1 jit_solution(14099614132261751291)
XLA Ops:
  0.6 0.0 copy-start
  0.6 0.0 copy-start.1
  0.7 0.0 copy-start.2
  0.7 0.0 copy-start.3
  0.7 0.0 copy-start.11
  0.7 2.9 %lead.1 = (f32[648,128]{1,0:T(8,128)}, f32[5,8,256]{2,1,0:T(8,128)}) custom-call(s32[1]{0:T(128)} %bitcast.late_ref, s32[10,256]{1,0:T(8,128)} %codes_ref.1, f32[256,640]{1,0:T(8,128)} %x_ref.5, f32[256,640]{1,0:T(8,128)} %dy_ref.5, f32[256,128]{1,0:T(8,128)} %b_ref.5, f32[256,128]{1,0:T(8,128)} %c_ref.5), custom_call_target="tpu_custom_call" | custom-call | flops 125829120 | bytes 1310720 | tf_op jit(solution)/shard_map/lead/pallas_call | solution.py:419
  3.6 0.0 copy-start.7
  3.6 2.1 %collective-permute-start = (f32[648,128]{1,0:T(8,128)}, f32[648,128]{1,0:T(8,128)S(1)}, u32[]{:S(2)}, u32[]{:S(2)}) collective-permute-start(f32[648,128]{1,0:T(8,128)} %get-tuple-element.28.sent_ref), channel_id=1, source_target_pairs={{0,8},{8,0},{16,24},{24,16},{32,40},{40,32},{48,56},{56,48},{64,72... | collective-permute-start | bytes 995336 | tf_op jit(solution)/shard_map/ppermute | solution.py:396
  5.7 0.0 copy-done
  5.7 1.2 %own.1.own_ref = f32[640,128]{1,0:T(8,128)S(1)} custom-call(s32[1]{0:T(128)} %bitcast.late_ref, s32[10,256]{1,0:T(8,128)S(1)} %copy-done.11, f32[256,640]{1,0:T(8,128)S(1)} %copy-done, f32[256,640]{1,0:T(8,128)S(1)} %copy-done.1, f32[256,128]{1,0:T(8,128)S(1)} %copy-done.2, f32[256,128]{1,0:T(8,128)S(1)} %copy-done.3), custom_call_target="tpu_custom_call" | custom-call | flops 125829120 | bytes 1966080 | tf_op jit(solution)/shard_map/own/pallas_call | solution.py:428
  6.9 0.6 collective-permute-done.got_ref
  7.5 0.9 %chip.1 = f32[32,24,128]{2,1,0:T(8,128)} custom-call(f32[640,128]{1,0:T(8,128)S(1)} %own.1.own_ref, f32[648,128]{1,0:T(8,128)S(1)} %copy-done.7, f32[648,128]{1,0:T(8,128)S(1)} %collective-permute-done.got_ref), custom_call_target="tpu_custom_call" | custom-call | flops 81920 | bytes 655360 | tf_op jit(solution)/shard_map/chip/pallas_call | solution.py:431
  8.5 12.7 %all-to-all-start = ((f32[32,24,128]{2,1,0:T(8,128)}), f32[32,24,128]{2,1,0:T(8,128)S(1)}, u32[]{:S(2)}, u32[]{:S(2)}) async-start(f32[32,24,128]{2,1,0:T(8,128)} %chip.1), calls=%async_computation | async-start | bytes 786432 | tf_op jit(solution)/shard_map/all_to_all | solution.py:401
  21.2 0.0 copy-start.4
  21.2 0.9 %copy-done.4 = f32[256,128]{1,0:T(8,128)S(1)} copy-done((f32[256,128]{1,0:T(8,128)S(1)}, f32[256,128]{1,0:T(8,128)}, u32[]{:S(2)}) %copy-start.4) | copy-done | bytes 131096
  22.1 7.3 %block.1 = (bf16[256,640]{1,0:T(8,128)(2,1)S(1)}, bf16[256,640]{1,0:T(8,128)(2,1)S(1)}, bf16[256,640]{1,0:T(8,128)(2,1)S(1)}, bf16[256,640]{1,0:T(8,128)(2,1)S(1...) custom-call(f32[5,8,256]{2,1,0:T(8,128)S(1)} %copy-done.12, ...), custom_call_target="tpu_custom_call" | custom-call | flops 1006632960 | bytes 3932160 | tf_op jit(solution)/shard_map/block/pallas_call | solution.py:443
  29.4 2.4 %all-to-all-done.got_ref = f32[32,24,128]{2,1,0:T(8,128)S(1)} async-done(((f32[32,24,128]{2,1,0:T(8,128)}), f32[32,24,128]{2,1,0:T(8,128)S(1)}, u32[]{:S(2)}, u32[]{:S(2)}) %all-to-all-start) | async-done | bytes 393248 | tf_op jit(solution)/shard_map/all_to_all | solution.py:401
  31.7 0.2 scan.1
  31.9 17.3 %all_to_all.15.back_ref = f32[32,5,4,128]{3,2,1,0:T(4,128)S(1)} all-to-all(f32[32,5,4,128]{3,2,1,0:T(4,128)S(1)} %scan.1), channel_id=1, replica_groups={{320,0,16,32,48,64,80,96,112,128,144,160,176,192,208,224,240,256,272,28..., dimensions={0} | all-to-all | bytes 655360 | tf_op jit(solution)/shard_map/all_to_all | solution.py:401
  49.3 2.0 %collective-permute-start.1 = (f32[32,5,4,128]{3,2,1,0:T(4,128)S(1)}, f32[32,5,4,128]{3,2,1,0:T(4,128)S(1)}, u32[]{:S(2)}, u32[]{:S(2)}) collective-permute-start(f32[32,5,4,128]{3,2,1,0:T(4,128)S(1)} %all_to_all.15.back_ref), channel_id=1, source_target_pairs={{0,8},{8,0},{16,24},{24,16},{32,40},{40,32},{48,56},{56,48},{64,72... | collective-permute-start | bytes 983048 | tf_op jit(solution)/shard_map/ppermute | solution.py:396
  51.3 0.9 %through.1 = (f32[640,128]{1,0:T(8,128)}, f32[256,128]{1,0:T(8,128)S(1)}) custom-call(s32[1]{0:T(128)} %bitcast.late_ref, f32[32,5,4,128]{3,2,1,0:T(4,128)S(1)} %all_to_all.15.back_ref, f32[648,128]{1,0:T(8,128)S(1)} %collective-permute-done.got_ref, bf16[256,640]{1,0:T(8,128)(2,1)S(1)} %get-tuple-element.38.xs_high, ...), custom_call_target="tpu_custom_call" | custom-call | flops 125829120 | bytes 1966080 | tf_op jit(solution)/shard_map/through/pallas_call | solution.py:459
  52.2 0.7 collective-permute-done.1.slab_ref.theirs_ref
  52.9 0.0 copy-done.9
  52.9 1.1 %rows.1 = f32[8,64,128]{2,1,0:T(8,128)} custom-call(s32[1]{0:T(128)} %bitcast.late_ref, f32[32,5,4,128]{3,2,1,0:T(4,128)S(1)} %collective-permute-done.1.slab_ref.theirs_ref, bf16[256,640]{1,0:T(8,128)(2,1)S(1)} %get-tuple-element.38.xs_high, bf16[256,640]{1,0:T(8,128)(2,1)S(1)} %get-tuple-element.39.xs_low, ...), custom_call_target="tpu_custom_call" | custom-call | flops 125829120 | bytes 1966080 | tf_op jit(solution)/shard_map/rows/pallas_call | solution.py:464
  54.0 0.0 copy-start.5
  54.1 10.6 %all-to-all-start.2 = ((f32[8,64,128]{2,1,0:T(8,128)}), f32[8,64,128]{2,1,0:T(8,128)S(1)}, u32[]{:S(2)}, u32[]{:S(2)}) async-start(f32[8,64,128]{2,1,0:T(8,128)} %rows.1), calls=%async_computation.2 | async-start | bytes 524288 | tf_op jit(solution)/shard_map/all_to_all | solution.py:472
  64.7 0.0 copy-done.8
  64.7 0.0 copy-start.6
  64.7 1.1 %copy-done.6 = f32[256,640]{1,0:T(8,128)S(1)} copy-done((f32[256,640]{1,0:T(8,128)S(1)}, f32[256,640]{1,0:T(8,128)}, u32[]{:S(2)}) %copy-start.6) | copy-done | bytes 655384
  65.8 3.2 %last.1 = (f32[256,640]{1,0:T(8,128)}, f32[10,256]{1,0:T(8,128)}) custom-call(s32[1]{0:T(128)} %bitcast.late_ref, f32[5,8,256]{2,1,0:T(8,128)S(1)} %copy-done.12, f32[640,128]{1,0:T(8,128)S(1)} %copy-done.8, f32[32,5,4,128]{3,2,1,0:T(4,128)S(1)} %collective-permute-done.1.slab_ref.theirs_ref, f32[256,640]{1,0:T(8,128)S(1)} %copy-done, ...), custom_call_target="tpu_custom_call" | custom-call | flops 251658240 | bytes 3932160 | tf_op jit(solution)/shard_map/last/pallas_call | solution.py:474
  69.0 4.4 %all-to-all-done.2 = f32[8,64,128]{2,1,0:T(8,128)S(1)} async-done(((f32[8,64,128]{2,1,0:T(8,128)}), f32[8,64,128]{2,1,0:T(8,128)S(1)}, u32[]{:S(2)}, u32[]{:S(2)}) %all-to-all-start.2) | async-done | bytes 262176 | tf_op jit(solution)/shard_map/all_to_all | solution.py:472
  73.4 0.6 fusion
  (15 shorter events, 0.0 us)
Async XLA Ops:
  0.6 5.1 %copy-start = (f32[256,640]{1,0:T(8,128)S(1)}, f32[256,640]{1,0:T(8,128)}, u32[]{:S(2)}) copy-start(f32[256,640]{1,0:T(8,128)} %x_ref.5) | copy-start | bytes 1966084
  0.6 5.1 %copy-start.1 = (f32[256,640]{1,0:T(8,128)S(1)}, f32[256,640]{1,0:T(8,128)}, u32[]{:S(2)}) copy-start(f32[256,640]{1,0:T(8,128)} %dy_ref.5) | copy-start | bytes 1966084
  0.7 5.1 %copy-start.2 = (f32[256,128]{1,0:T(8,128)S(1)}, f32[256,128]{1,0:T(8,128)}, u32[]{:S(2)}) copy-start(f32[256,128]{1,0:T(8,128)} %b_ref.5) | copy-start | bytes 393220
  0.7 5.1 %copy-start.3 = (f32[256,128]{1,0:T(8,128)S(1)}, f32[256,128]{1,0:T(8,128)}, u32[]{:S(2)}) copy-start(f32[256,128]{1,0:T(8,128)} %c_ref.5) | copy-start | bytes 393220
  0.7 5.1 %copy-start.11 = (s32[10,256]{1,0:T(8,128)S(1)}, s32[10,256]{1,0:T(8,128)}, u32[]{:S(2)}) copy-start(s32[10,256]{1,0:T(8,128)} %codes_ref.1) | copy-start | bytes 30724
  3.6 3.9 %copy-start.7 = (f32[648,128]{1,0:T(8,128)S(1)}, f32[648,128]{1,0:T(8,128)}, u32[]{:S(2)}) copy-start(f32[648,128]{1,0:T(8,128)} %get-tuple-element.28.sent_ref) | copy-start | bytes 995332
  3.6 3.9 %collective-permute-start = (f32[648,128]{1,0:T(8,128)}, f32[648,128]{1,0:T(8,128)S(1)}, u32[]{:S(2)}, u32[]{:S(2)}) collective-permute-start(f32[648,128]{1,0:T(8,128)} %get-tuple-element.28.sent_ref), channel_id=1, source_target_pairs={{0,8},{8,0},{16,24},{24,16},{32,40},{40,32},{48,56},{56,48},{64,72... | collective-permute-start | bytes 995336 | tf_op jit(solution)/shard_map/ppermute | solution.py:396
  8.4 12.7 %copy-start.12 = (f32[5,8,256]{2,1,0:T(8,128)S(1)}, f32[5,8,256]{2,1,0:T(8,128)}, u32[]{:S(2)}) copy-start(f32[5,8,256]{2,1,0:T(8,128)} %get-tuple-element.27.pairs_ref) | copy-start | bytes 122884
  8.5 23.3 %all-to-all-start = ((f32[32,24,128]{2,1,0:T(8,128)}), f32[32,24,128]{2,1,0:T(8,128)S(1)}, u32[]{:S(2)}, u32[]{:S(2)}) async-start(f32[32,24,128]{2,1,0:T(8,128)} %chip.1), calls=%async_computation | async-start | bytes 786432 | tf_op jit(solution)/shard_map/all_to_all | solution.py:401
  21.2 0.9 %copy-start.4 = (f32[256,128]{1,0:T(8,128)S(1)}, f32[256,128]{1,0:T(8,128)}, u32[]{:S(2)}) copy-start(f32[256,128]{1,0:T(8,128)} %c_ref.5) | copy-start | bytes 393220
  49.2 3.6 %copy-start.9 = (f32[256,128]{1,0:T(8,128)S(1)}, f32[256,128]{1,0:T(8,128)}, u32[]{:S(2)}) copy-start(f32[256,128]{1,0:T(8,128)} %get-tuple-element.47.db_ref) | copy-start | bytes 393220
  49.3 3.7 %copy-start.10 = (f32[256,128]{1,0:T(8,128)S(1)}, f32[256,128]{1,0:T(8,128)}, u32[]{:S(2)}) copy-start(f32[256,128]{1,0:T(8,128)} %get-tuple-element.48.dc_ref) | copy-start | bytes 393220
  49.3 3.6 %collective-permute-start.1 = (f32[32,5,4,128]{3,2,1,0:T(4,128)S(1)}, f32[32,5,4,128]{3,2,1,0:T(4,128)S(1)}, u32[]{:S(2)}, u32[]{:S(2)}) collective-permute-start(f32[32,5,4,128]{3,2,1,0:T(4,128)S(1)} %all_to_all.15.back_ref), channel_id=1, source_target_pairs={{0,8},{8,0},{16,24},{24,16},{32,40},{40,32},{48,56},{56,48},{64,72... | collective-permute-start | bytes 983048 | tf_op jit(solution)/shard_map/ppermute | solution.py:396
  54.0 10.6 %copy-start.5 = (f32[256,128]{1,0:T(8,128)S(1)}, f32[256,128]{1,0:T(8,128)}, u32[]{:S(2)}) copy-start(f32[256,128]{1,0:T(8,128)} %c_ref.5) | copy-start | bytes 393220
  54.0 10.6 %copy-start.8 = (f32[640,128]{1,0:T(8,128)S(1)}, f32[640,128]{1,0:T(8,128)}, u32[]{:S(2)}) copy-start(f32[640,128]{1,0:T(8,128)} %get-tuple-element.42.through_ref) | copy-start | bytes 983044
  54.1 10.6 %copy-start.13 = (f32[5,8,256]{2,1,0:T(8,128)S(1)}, f32[5,8,256]{2,1,0:T(8,128)}, u32[]{:S(2)}) copy-start(f32[5,8,256]{2,1,0:T(8,128)} %get-tuple-element.44.pair_ref) | copy-start | bytes 122884
  54.1 19.4 %all-to-all-start.2 = ((f32[8,64,128]{2,1,0:T(8,128)}), f32[8,64,128]{2,1,0:T(8,128)S(1)}, u32[]{:S(2)}, u32[]{:S(2)}) async-start(f32[8,64,128]{2,1,0:T(8,128)} %rows.1), calls=%async_computation.2 | async-start | bytes 524288 | tf_op jit(solution)/shard_map/all_to_all | solution.py:472
  64.7 1.1 %copy-start.6 = (f32[256,640]{1,0:T(8,128)S(1)}, f32[256,640]{1,0:T(8,128)}, u32[]{:S(2)}) copy-start(f32[256,640]{1,0:T(8,128)} %get-tuple-element.43.near_ref) | copy-start | bytes 1966084
